TPU v7x, 32 devices: a whole 2x2x4 slice. The times are simulated.
32 devices in a mesh: groups: 2 (over y), member: 2 (over core), fsdp: 8 (over z, x).
Axes of the slice: x: 2, y: 2, z: 4, core: 2. Of those that a mesh axis runs over, the one named last changes fastest.
Arguments:
- features: bfloat16 [16, 128, 4096], P(('groups', 'fsdp')), parts along dimension 0, may hold values from -6 to 6
- blocks: int32 [4, 2], P(('groups', 'member')), parts along dimension 0, may hold values from 0 to 7
- pair_labels: int32 [4, 4, 2], P(('groups', 'member')), parts along dimension 0, may hold values from 0 to 1, as said below
- ffn_gain: float32 [2, 4096], P('member'), may hold values from 0.5 to 2
- final_gain: float32 [2, 4096], P('member'), may hold values from 0.5 to 2
- score_head: float32 [2, 4096], P('member'), may hold values from -0.75 to 0.75
- w_gate: bfloat16 [2, 4096, 14336], P('member', None, 'fsdp'), may hold values from -0.09375 to 0.09375
- w_up: bfloat16 [2, 4096, 14336], P('member', None, 'fsdp'), may hold values from -1 to 1
- w_down: bfloat16 [2, 14336, 4096], P('member', 'fsdp'), may hold values from -1 to 1
Outputs:
- pair_loss: float32 [4], P(('groups', 'member')), parts along dimension 0
- grad_gate: bfloat16 [4, 4096, 14336], P(('groups', 'member'), None, 'fsdp'), parts along dimension 0
- grad_up: bfloat16 [4, 4096, 14336], P(('groups', 'member'), None, 'fsdp'), parts along dimension 0
- grad_down: bfloat16 [4, 14336, 4096], P(('groups', 'member'), 'fsdp'), parts along dimension 0
- grad_head: float32 [4, 4096], P(('groups', 'member'), 'fsdp'), parts along dimension 0
- grad_final_gain: float32 [4, 4096], P(('groups', 'member'), 'fsdp'), parts along dimension 0
- grad_ffn_gain: float32 [4, 4096], P(('groups', 'member'), 'fsdp'), parts along dimension 0
- grad_features: bfloat16 [16, 128, 4096], P(('groups', 'fsdp')), parts along dimension 0
There are 2 independent parts, one for each index of `groups`. A program takes and returns all parts, laid end to end along the dimension named above; an argument that names none is the same for every part. Nothing has to cross between parts.
Inputs may be any that keep to these rules, and one draw needn't show every extreme that they name: `pair_labels`: in every pair the chosen and the rejected entry differ.
All inputs are finite; a program needn't handle non-finite values.
Results may differ from a plain program's by a relative error of at most 0.008.
Values may be sent and summed in bfloat16 or wider, within the bound.
No kernel may reach another device: no remote copies, remote signals or barrier semaphores. Data moves between devices by JAX's collectives and lax.ppermute only.
A program may use at most 256 MiB of HBM per device.

v0:
```python
import jax
import jax.numpy as jnp
from jax import lax
from jax.sharding import PartitionSpec as P

eps = 1e-05
loss_scale = 256.0


def pair_terms(scores, pair_rows, entries, block_len):
    reward = jnp.mean(scores.reshape(entries, block_len), axis=1)
    slots = jnp.arange(entries, dtype=jnp.int32)
    select = (pair_rows[:, 0:1] == slots[None, :]).astype(jnp.float32) - (
        pair_rows[:, 1:2] == slots[None, :]
    ).astype(jnp.float32)
    margin = jnp.sum(select * reward[None, :], axis=1)
    total_loss = jnp.sum(jax.nn.softplus(-margin))
    weights = -jax.nn.sigmoid(-margin) * loss_scale
    dreward = jnp.sum(select * weights[:, None], axis=0)
    dscore = jnp.repeat(dreward / block_len, block_len, total_repeat_length=entries * block_len)
    return (total_loss, dscore)


def contract(left, right, left_dim, right_dim):
    return lax.dot_general(
        left, right, (((left_dim,), (right_dim,)), ((), ())), preferred_element_type=jnp.float32
    )


def body(features, blocks, pair_labels, ffn_gain, final_gain, score_head, w_gate, w_up, w_down):
    nodes = lax.axis_size("fsdp")
    position = lax.axis_index("fsdp")
    owned_count = features.shape[0]
    block_len = features.shape[1]
    model_width = features.shape[2]
    columns = model_width // nodes
    start = position * columns
    chosen_blocks = blocks[0]
    entries = chosen_blocks.shape[0]
    row_count = entries * block_len
    owner = chosen_blocks // owned_count
    local_index = chosen_blocks - owner * owned_count
    is_mine = owner == position
    picked = jnp.take(features, local_index, axis=0)
    outgoing = jnp.where(is_mine[:, None, None], picked, jnp.zeros_like(picked))
    arrived = lax.all_to_all(outgoing[None], "fsdp", split_axis=3, concat_axis=0, tiled=True)
    bands = jnp.sum(arrived, axis=0, dtype=jnp.float32).astype(jnp.bfloat16)
    gathered = lax.all_gather(bands, "fsdp", axis=2, tiled=True)
    inputs = gathered.reshape(row_count, model_width).astype(jnp.float32)
    inverse_in = lax.rsqrt(jnp.mean(inputs * inputs, axis=1, keepdims=True) + eps)
    normed_in = inputs * inverse_in
    scaled_in = (normed_in * ffn_gain[0][None, :]).astype(jnp.bfloat16)
    gate_pre = jnp.dot(scaled_in, w_gate[0], preferred_element_type=jnp.float32)
    up_pre = jnp.dot(scaled_in, w_up[0], preferred_element_type=jnp.float32)
    silu_gate = jax.nn.silu(gate_pre)
    hidden = (silu_gate * up_pre).astype(jnp.bfloat16)
    out_part = jnp.dot(hidden, w_down[0], preferred_element_type=jnp.float32)
    gain_head = final_gain[0] * score_head[0]
    final_share = lax.dynamic_slice_in_dim(final_gain[0], start, columns, 0)
    head_share = lax.dynamic_slice_in_dim(score_head[0], start, columns, 0)
    ffn_share = lax.dynamic_slice_in_dim(ffn_gain[0], start, columns, 0)
    normed_in_share = lax.dynamic_slice_in_dim(normed_in, start, columns, 1)
    out_total = lax.psum(out_part, "fsdp")
    summed = inputs + out_total
    inverse_out = lax.rsqrt(jnp.mean(summed * summed, axis=1, keepdims=True) + eps)
    normed_out = summed * inverse_out
    scores = jnp.sum(normed_out * gain_head[None, :], axis=1)
    total_loss, dscore = pair_terms(scores, pair_labels[0], entries, block_len)
    dsummed = inverse_out * (
        dscore[:, None] * gain_head[None, :] - normed_out * (dscore * scores / model_width)[:, None]
    )
    dsummed_b = dsummed.astype(jnp.bfloat16)
    normed_share = lax.dynamic_slice_in_dim(normed_out, start, columns, 1)
    dsummed_share = lax.dynamic_slice_in_dim(dsummed, start, columns, 1)
    weighted = jnp.sum(dscore[:, None] * normed_share, axis=0)
    grad_head = final_share * weighted
    grad_final = head_share * weighted
    grad_down = contract(hidden, dsummed_b, 0, 0).astype(jnp.bfloat16)
    dhidden = contract(dsummed_b, w_down[0], 1, 1)
    sigmoid_gate = jax.nn.sigmoid(gate_pre)
    grad_gate_pre = (
        dhidden * up_pre * sigmoid_gate * (1.0 + gate_pre * (1.0 - sigmoid_gate))
    ).astype(jnp.bfloat16)
    grad_up_pre = (dhidden * silu_gate).astype(jnp.bfloat16)
    grad_gate = contract(scaled_in, grad_gate_pre, 0, 0).astype(jnp.bfloat16)
    grad_up = contract(scaled_in, grad_up_pre, 0, 0).astype(jnp.bfloat16)
    dscaled_part = contract(grad_gate_pre, w_gate[0], 1, 1) + contract(grad_up_pre, w_up[0], 1, 1)
    dscaled_share = lax.psum_scatter(dscaled_part, "fsdp", scatter_dimension=1, tiled=True)
    grad_ffn = jnp.sum(dscaled_share * normed_in_share, axis=0)
    dnormed_share = dscaled_share * ffn_share[None, :]
    row_inner = lax.psum(jnp.sum(dnormed_share * normed_in_share, axis=1), "fsdp")
    drows_share = (
        inverse_in * (dnormed_share - normed_in_share * (row_inner / model_width)[:, None])
        + dsummed_share
    )
    drows_share = drows_share.astype(jnp.bfloat16).reshape(entries, block_len, columns)
    owners = jnp.arange(nodes, dtype=jnp.int32)
    to_owner = owner[None, :] == owners[:, None]
    outgoing_back = jnp.where(
        to_owner[:, :, None, None], drows_share[None], jnp.zeros_like(drows_share[None])
    )
    returned = lax.all_to_all(outgoing_back, "fsdp", split_axis=0, concat_axis=3, tiled=True)[0]
    owner_hit = (
        (local_index[None, :] == jnp.arange(owned_count, dtype=jnp.int32)[:, None])
        & is_mine[None, :]
    ).astype(jnp.bfloat16)
    partial_grad = jnp.einsum(
        "kl,lbd->kbd", owner_hit, returned, preferred_element_type=jnp.float32
    )
    total_grad = lax.psum(partial_grad.astype(jnp.bfloat16), "member")
    return (
        total_loss.reshape(1),
        grad_gate[None],
        grad_up[None],
        grad_down[None],
        grad_head[None],
        grad_final[None],
        grad_ffn[None],
        total_grad,
    )


def solution(mesh):
    in_specs = (
        P(("groups", "fsdp"), None, None),
        P(("groups", "member"), None),
        P(("groups", "member"), None, None),
        P("member", None),
        P("member", None),
        P("member", None),
        P("member", None, "fsdp"),
        P("member", None, "fsdp"),
        P("member", "fsdp", None),
    )
    out_specs = (
        P(("groups", "member")),
        P(("groups", "member"), None, "fsdp"),
        P(("groups", "member"), None, "fsdp"),
        P(("groups", "member"), "fsdp", None),
        P(("groups", "member"), "fsdp"),
        P(("groups", "member"), "fsdp"),
        P(("groups", "member"), "fsdp"),
        P(("groups", "fsdp"), None, None),
    )
    return jax.shard_map(body, mesh=mesh, in_specs=in_specs, out_specs=out_specs, check_vma=False)
```

profile of v0, /device:TPU:0, one launch (start us, length us, event | category | flops | bytes accessed | tf_op | source)
XLA Modules:
  0.0 576.1 jit_solution(16687666453106717526)
XLA Ops:
  7.2 0.0 all-gather.2.cloned.1.call-start
  7.2 1.6 copy.29
  8.8 0.7 broadcast_compare_fusion
  9.5 2.3 broadcast_select_fusion
  11.8 0.0 copy-start.8
  11.8 55.3 %all_to_all.27 = bf16[1,2,128,4096]{2,1,0,3:T(2,128)(2,1)S(1)} all-to-all(bf16[1,2,128,4096]{2,1,0,3:T(2,128)(2,1)S(1)} %broadcast_select_fusion), channel_id=1, replica_groups=mesh['groups'=2,'member'=2,'fsdp'=8] {'fsdp'}, dimensions={3} | all-to-all | bytes 4194304 | tf_op jit(solution)/shard_map/all_to_all | solution.py:46
  67.1 3.2 reduce_sum.104
  70.3 0.0 all-gather.2.cloned.1.call-update
  70.3 0.5 all-reduce.3.cloned.1.call-start
  70.8 48.0 %all-gather.2.cloned.1.call-done = bf16[2,128,4096]{1,0,2:T(2,128)(2,1)} async-done(((bf16[2,128,512]{1,0,2:T(2,128)(2,1)}), bf16[2,128,4096]{1,0,2:T(2,128)(2,1)}) %all-gather.2.cloned.1.call-update) | async-done | bytes 2097168 | tf_op jit(solution)/shard_map/all_gather | solution.py:48
  118.8 5.4 multiply_reduce_fusion.2
  124.2 12.9 %multiply_convert_fusion.1 = bf16[2,128,4096]{1,0,2:T(2,128)(2,1)S(1)} fusion(f32[4096]{0:T(1024)S(1)} %bitcast.107, bf16[2,128,4096]{1,0,2:T(2,128)(2,1)} %all-gather.2.cloned.1.call-done, f32[2,128]{1,0:T(2,128)S(1)} %get-tuple-element.32), kind=kLoop, calls=%fused_computation.25 | loop fusion | flops 4194304 | bytes 4211712 | tf_op jit(solution)/shard_map/convert_element_type | solution.py:52
  137.1 0.0 slice-start
  137.1 0.0 slice-start.1
  137.1 8.1 %fusion.10 = f32[256,1792]{1,0:T(8,128)S(1)} fusion(bf16[1,4096,1792]{2,1,0:T(8,128)(2,1)} %param.17, bf16[512,8,2,128]{3,2,1,0:T(2,128)(2,1)S(1)} %bitcast.101), kind=kOutput, calls=%fused_computation.13 | convolution fusion | flops 3758096384 | bytes 18612224 | tf_op jit(solution)/shard_map/dot_general | solution.py:53
  145.2 0.0 slice-start.2
  145.2 0.0 slice-start.3
  145.2 11.3 %multiply_convert_fusion.4 = (bf16[256,1792]{1,0:T(8,128)(2,1)S(1)}, f32[256,1792]{1,0:T(8,128)}) fusion(f32[256,1792]{1,0:T(8,128)S(1)} %fusion.10, bf16[1,4096,1792]{2,1,0:T(8,128)(2,1)} %param.18, bf16[512,8,2,128]{3,2,1,0:T(2,128)(2,1)S(1)} %bitcast.102), kind=kOutput, calls=%fused_computation.37 | convolution fusion | flops 3760848896 | bytes 21364736 | tf_op jit(solution)/shard_map/dot_general | solution.py:54
  156.6 5.5 fusion.2
  162.1 0.0 all-reduce.3.cloned.1.call-update
  162.1 0.2 reduce-scatter.2.cloned.1.call-start
  162.3 0.5 copy-done.9
  162.8 0.0 copy-done.10
  162.9 0.8 copy-done.3
  163.7 4.1 copy.30
  167.8 149.2 %all-reduce.3.cloned.1.call-done = f32[256,4096]{1,0:T(8,128)} async-done(((f32[256,4096]{1,0:T(8,128)}), f32[256,4096]{1,0:T(8,128)}) %all-reduce.3.cloned.1.call-update) | async-done | bytes 4194320 | tf_op jit(solution)/shard_map/psum | solution.py:63
  317.1 4.1 multiply_reduce_fusion.1
  321.2 0.5 copy-done.1
  321.7 1.3 copy-done.4
  323.0 3.0 multiply_reduce_fusion
  325.9 0.1 bitcast_reduce_fusion
  326.1 0.1 multiply_reduce_fusion.7
  326.2 0.9 negate_multiply_fusion
  327.0 0.1 multiply_reduce_fusion.6
  327.1 0.7 fusion.33
  327.8 1.3 compare_select_fusion.1
  329.2 2.9 subtract_multiply_fusion
  332.1 12.5 %multiply_convert_fusion.2 = (bf16[256,1792]{1,0:T(8,128)(2,1)}, bf16[256,1792]{1,0:T(8,128)(2,1)}) fusion(f32[256,1792]{1,0:T(8,128)S(1)} %copy-done.6, f32[256,1792]{1,0:T(8,128)} %get-tuple-element.40, bf16[1,1792,4096]{2,1,0:T(8,128)(2,1)} %param.19, f32[256,4096]{1,0:T(8,128)} %subtract_multiply_fusion), kind=kOutput, calls=%fused_computation.35 | convolution fusion | flops 3765108736 | bytes 24379392 | tf_op jit(solution)/shard_map/dot_general | solution.py:25
  344.6 11.5 %fusion.4 = f32[256,4096]{1,0:T(8,128)} fusion(bf16[256,1792]{1,0:T(8,128)(2,1)} %get-tuple-element.27, bf16[1,4096,1792]{2,1,0:T(8,128)(2,1)} %param.18), kind=kOutput, calls=%fused_computation.7 | convolution fusion | flops 3758096384 | bytes 19791872 | tf_op jit(solution)/shard_map/dot_general | solution.py:25
  356.1 17.0 %fusion.15 = f32[256,4096]{1,0:T(8,128)} fusion(f32[256,4096]{1,0:T(8,128)} %fusion.4, bf16[256,1792]{1,0:T(8,128)(2,1)S(1)} %copy-done.7, bf16[1,4096,1792]{2,1,0:T(8,128)(2,1)} %param.17), kind=kOutput, calls=%fused_computation.18 | convolution fusion | flops 3759144960 | bytes 23986176 | tf_op jit(solution)/shard_map/dot_general | solution.py:25
  373.1 0.0 copy-start.12
  373.1 0.0 reduce-scatter.2.cloned.1.call-update
  373.2 0.6 copy-done.12
  373.8 87.0 %reduce-scatter.2.cloned.1.call-done = f32[256,512]{1,0:T(8,128)} async-done(((f32[256,4096]{1,0:T(8,128)}), f32[256,512]{1,0:T(8,128)}) %reduce-scatter.2.cloned.1.call-update) | async-done | bytes 524304 | tf_op jit(solution)/shard_map/reduce_scatter | solution.py:88
  460.8 2.0 multiply_reduce_fusion.3
  462.8 20.1 %psum.22 = f32[256]{0:T(256)S(1)} all-reduce(f32[256]{0:T(256)S(1)} %get-tuple-element.20), channel_id=1, replica_groups=mesh['groups'=2,'member'=2,'fsdp'=8] {'fsdp'}, use_global_device_ids=true, to_apply=%region_13.14 | all-reduce | flops 256 | bytes 2048 | tf_op jit(solution)/shard_map/psum | solution.py:91
  482.9 1.5 add_convert_fusion
  484.4 0.2 copy.31
  484.6 1.5 broadcast_select_fusion.1
  486.1 3.6 all-to-all-start.1
  489.7 0.0 all-reduce.5.cloned.1.call-start
  489.8 12.0 %fusion.12 = bf16[1,4096,1792]{2,1,0:T(8,128)(2,1)} fusion(bf16[256,1792]{1,0:T(8,128)(2,1)} %get-tuple-element.28, f32[256,4096]{1,0:T(8,128)} %get-tuple-element.26, f32[4096]{0:T(1024)S(1)} %bitcast.108), kind=kOutput, calls=%fused_computation.15 | convolution fusion | flops 3767533568 | bytes 19808256 | tf_op jit(solution)/shard_map/dot_general | solution.py:25
  501.8 33.1 %all-to-all-done.1 = bf16[8,2,128,512]{2,3,1,0:T(8,128)(2,1)S(1)} async-done(((bf16[8,2,128,512]{2,3,1,0:T(8,128)(2,1)}), bf16[8,2,128,512]{2,3,1,0:T(8,128)(2,1)S(1)}, u32[]{:S(2)}, u32[]{:S(2)}) %all-to-all-start.1) | async-done | bytes 2097184 | tf_op jit(solution)/shard_map/all_to_all | solution.py:102
  534.9 1.5 copy.32
  536.3 5.0 copy.33
  541.4 2.3 fusion.26
  543.7 2.1 copy.49
  545.8 0.0 all-reduce.5.cloned.1.call-update
  545.8 0.0 copy-start
  545.8 9.9 %fusion.14 = bf16[1,1792,4096]{2,1,0:T(8,128)(2,1)} fusion(bf16[256,1792]{1,0:T(8,128)(2,1)S(1)} %get-tuple-element.39, f32[256,4096]{1,0:T(8,128)} %subtract_multiply_fusion), kind=kOutput, calls=%fused_computation.17 | convolution fusion | flops 3766484992 | bytes 19791872 | tf_op jit(solution)/shard_map/dot_general | solution.py:25
  555.8 1.2 multiply_reduce_fusion.5
  556.9 1.3 dynamic-slice_multiply_fusion
  558.2 8.8 %fusion.13 = bf16[1,4096,1792]{2,1,0:T(8,128)(2,1)} fusion(bf16[256,1792]{1,0:T(8,128)(2,1)} %get-tuple-element.27, f32[256,4096]{1,0:T(8,128)S(1)} %copy-done, f32[4096]{0:T(1024)S(1)} %bitcast.109), kind=kOutput, calls=%fused_computation.16 | convolution fusion | flops 3767533568 | bytes 19808256 | tf_op jit(solution)/shard_map/dot_general | solution.py:25
  567.0 2.3 copy.52
  (35 shorter events, 0.1 us)
Async XLA Ops:
  7.2 111.6 %all-gather.2.cloned.1.call-start = ((), (), s32[]{:S(2)}) async-start(), calls=%async_computation.3 | async-start | bytes 2359296 | tf_op jit(solution)/shard_map/all_gather | solution.py:48
  11.8 112.4 %copy-start.8 = (f32[1,4096]{1,0:T(1,128)S(1)}, f32[1,4096]{1,0:T(1,128)}, u32[]{:S(2)}) copy-start(f32[1,4096]{1,0:T(1,128)} %param.14) | copy-start | bytes 49156
  70.3 246.7 %all-reduce.3.cloned.1.call-start = ((), (), s32[]{:S(2)}) async-start(), calls=%async_computation.4 | async-start | bytes 8388608 | tf_op jit(solution)/shard_map/psum | solution.py:63
  137.1 19.5 %slice-start = ((s8[14680064]{0:T(1024)(128)(4,1)}), s8[4194304]{0:T(1024)(128)(4,1)S(1)}, s32[]{:S(2)}) async-start(s8[14680064]{0:T(1024)(128)(4,1)} %bitcast.120), calls=%async_computation.7 | async-start | bytes 8388608
  137.1 19.5 %slice-start.1 = ((s8[14680064]{0:T(1024)(128)(4,1)}), s8[4194304]{0:T(1024)(128)(4,1)S(1)}, s32[]{:S(2)}) async-start(s8[14680064]{0:T(1024)(128)(4,1)} %bitcast.120), calls=%async_computation.8 | async-start | bytes 8388608
  145.2 11.4 %copy-start.5 = (f32[256,1792]{1,0:T(8,128)}, f32[256,1792]{1,0:T(8,128)S(1)}, u32[]{:S(2)}) copy-start(f32[256,1792]{1,0:T(8,128)S(1)} %fusion.10) | copy-start | bytes 5505028
  145.2 11.4 %slice-start.2 = ((s8[14680064]{0:T(1024)(128)(4,1)}), s8[4194304]{0:T(1024)(128)(4,1)S(1)}, s32[]{:S(2)}) async-start(s8[14680064]{0:T(1024)(128)(4,1)} %bitcast.120), calls=%async_computation.9 | async-start | bytes 8388608
  145.2 11.4 %slice-start.3 = ((s8[14680064]{0:T(1024)(128)(4,1)}), s8[2097152]{0:T(1024)(128)(4,1)S(1)}, s32[]{:S(2)}) async-start(s8[14680064]{0:T(1024)(128)(4,1)} %bitcast.120), calls=%async_computation.10 | async-start | bytes 4194304
  162.1 0.7 copy-start.9
  162.1 0.7 copy-start.10
  162.1 0.8 copy-start.11
  162.1 1.6 copy-start.3
  162.1 298.7 %reduce-scatter.2.cloned.1.call-start = ((), (), s32[]{:S(2)}) async-start(), calls=%async_computation.5 | async-start | bytes 4718592 | tf_op jit(solution)/shard_map/reduce_scatter | solution.py:88
  317.1 4.6 copy-start.1
  317.1 5.9 %copy-start.4 = (f32[256,4096]{1,0:T(8,128)S(1)}, f32[256,4096]{1,0:T(8,128)}, u32[]{:S(2)}) copy-start(f32[256,4096]{1,0:T(8,128)} %all-reduce.3.cloned.1.call-done) | copy-start | bytes 12582916
  325.9 6.1 %copy-start.2 = (f32[256,4096]{1,0:T(8,128)}, f32[256,4096]{1,0:T(8,128)S(1)}, u32[]{:S(2)}) copy-start(f32[256,4096]{1,0:T(8,128)S(1)} %get-tuple-element.25) | copy-start | bytes 12582916
  329.2 2.9 copy-start.6
  344.6 11.5 %copy-start.7 = (bf16[256,1792]{1,0:T(8,128)(2,1)S(1)}, bf16[256,1792]{1,0:T(8,128)(2,1)}, u32[]{:S(2)}) copy-start(bf16[256,1792]{1,0:T(8,128)(2,1)} %get-tuple-element.28) | copy-start | bytes 2752516
  373.1 0.7 copy-start.12
  486.1 48.7 %all-to-all-start.1 = ((bf16[8,2,128,512]{2,3,1,0:T(8,128)(2,1)}), bf16[8,2,128,512]{2,3,1,0:T(8,128)(2,1)S(1)}, u32[]{:S(2)}, u32[]{:S(2)}) async-start(bf16[8,2,128,512]{2,3,1,0:T(8,128)(2,1)} %broadcast_select_fusion.1), calls=%async_computation.2 | async-start | bytes 4194304 | tf_op jit(solution)/shard_map/all_to_all | solution.py:102
  489.7 77.3 %all-reduce.5.cloned.1.call-start = ((), (), s32[]{:S(2)}) async-start(), calls=%async_computation.6 | async-start | bytes 2097152 | tf_op jit(solution)/shard_map/psum | solution.py:110
  545.8 12.4 %copy-start = (f32[256,4096]{1,0:T(8,128)S(1)}, f32[256,4096]{1,0:T(8,128)}, u32[]{:S(2)}) copy-start(f32[256,4096]{1,0:T(8,128)} %get-tuple-element.26) | copy-start | bytes 12582916
Sparse Core Ops, SparseCore 0:
  70.5 48.3 all-gather.1
  162.2 154.7 all-reduce.2
  373.3 87.4 reduce-scatter.1
  546.0 18.4 all-reduce.4
where the time goes:
time: 580 us; the launch traced here: 576 us
  waiting for transfers between devices  317 us (55%)
  matrix products  98.9 us (17%)
  blocking collectives  75.4 us (13%)
  other arithmetic  44.3 us (8%)
  local copies, waits for them, and re-layouts  21.3 us (4%)
  between operations  14.3 us (2%)
    psum x1, waiting for transfers between devices, body(): out_total = lax.psum(out_part, 'fsdp')  149 us
    reduce_scatter x1, waiting for transfers between devices, body(): lax.psum_scatter(dscaled_part, 'fsdp', scatter_dimension=1, tiled=True)  87 us
    dot_general x6, matrix products, contract(): lax.dot_general(left, right, (((left_dim,), (right_dim,)), ((), ())), pre...  71.7 us
    all_to_all x1, blocking collectives, body(): lax.all_to_all(outgoing[None], 'fsdp', split_axis=3, concat_axis=0, tiled...  55.3 us
    all_gather x1, waiting for transfers between devices, body(): gathered = lax.all_gather(bands, 'fsdp', axis=2, tiled=True)  48 us
    all_to_all x1, waiting for transfers between devices, body(): lax.all_to_all(outgoing_back, 'fsdp', split_axis=0, concat_axis=3, tiled=...  33.1 us
    psum x1, blocking collectives, body(): lax.psum(jnp.sum(dnormed_share * normed_in_share, axis=1), 'fsdp')  20.1 us
    convert_element_type x1, other arithmetic, body(): scaled_in = (normed_in * ffn_gain[0][None, :]).astype(jnp.bfloat16)  12.9 us
  transfers between devices with their start and end apart: 5, of which 4 were waited for; matrix products, arithmetic and copies ran while one was open for 6% of the time, Pallas kernels for 0%

commit v1 on v0

--- a/solution.py
+++ b/solution.py
@@ -60,7 +60,11 @@
     head_share = lax.dynamic_slice_in_dim(score_head[0], start, columns, 0)
     ffn_share = lax.dynamic_slice_in_dim(ffn_gain[0], start, columns, 0)
     normed_in_share = lax.dynamic_slice_in_dim(normed_in, start, columns, 1)
-    out_total = lax.psum(out_part, "fsdp")
+    out_total = out_part
+    for hop in (1, 2, 4):
+        out_total = out_total + lax.ppermute(
+            out_total, "fsdp", [(dev, dev ^ hop) for dev in range(8)]
+        )
     summed = inputs + out_total
     inverse_out = lax.rsqrt(jnp.mean(summed * summed, axis=1, keepdims=True) + eps)
     normed_out = summed * inverse_out

time: 580 us -> 798 us (1.38)
  waiting for transfers between devices: 317 us -> 523 us
  other arithmetic: 44.3 us -> 52.7 us
    ppermute x0 -> x3, waiting for transfers between devices: none -> 353 us  [body(): lax.ppermute(out_total, 'fsdp', [(dev, dev ^ hop) for dev in range(8)])]
    psum x1 -> x0, waiting for transfers between devices: 149 us -> none  [body(): out_total = lax.psum(out_part, 'fsdp')]
  transfers between devices with their start and end apart: 5 -> 7, of which waited for: 4 -> 6; matrix products, arithmetic and copies ran while one was open for 6% -> 5% of each run, Pallas kernels for 0% -> 0%
where the time goes in v1:
time: 798 us; the launch traced here: 791 us
  waiting for transfers between devices  523 us (66%)
  matrix products  97.8 us (12%)
  blocking collectives  75.4 us (9%)
  other arithmetic  52.7 us (7%)
  local copies, waits for them, and re-layouts  18.9 us (2%)
  between operations  14.3 us (2%)
  starting transfers between devices  8.94 us (1%)
    ppermute x3, waiting for transfers between devices, body(): lax.ppermute(out_total, 'fsdp', [(dev, dev ^ hop) for dev in range(8)])  353 us
    reduce_scatter x1, waiting for transfers between devices, body(): lax.psum_scatter(dscaled_part, 'fsdp', scatter_dimension=1, tiled=True)  88.2 us
    dot_general x6, matrix products, contract(): lax.dot_general(left, right, (((left_dim,), (right_dim,)), ((), ())), pre...  71.7 us
    all_to_all x1, blocking collectives, body(): lax.all_to_all(outgoing[None], 'fsdp', split_axis=3, concat_axis=0, tiled...  55.3 us
    all_gather x1, waiting for transfers between devices, body(): gathered = lax.all_gather(bands, 'fsdp', axis=2, tiled=True)  48.4 us
    all_to_all x1, waiting for transfers between devices, body(): lax.all_to_all(outgoing_back, 'fsdp', split_axis=0, concat_axis=3, tiled=...  33.1 us
    psum x1, blocking collectives, body(): lax.psum(jnp.sum(dnormed_share * normed_in_share, axis=1), 'fsdp')  20.1 us
  transfers between devices with their start and end apart: 7, of which 6 were waited for; matrix products, arithmetic and copies ran while one was open for 5% of the time, Pallas kernels for 0%

profile of v1, /device:TPU:0, one launch (start us, length us, event | category | flops | bytes accessed | tf_op | source)
XLA Modules:
  0.0 791.0 jit_solution(567537601005845803)
XLA Ops:
  7.2 0.0 all-gather.2.cloned.1.call-start
  7.2 1.6 copy.29
  8.8 0.7 broadcast_compare_fusion
  9.5 2.3 broadcast_select_fusion
  11.8 0.0 copy-start.7
  11.8 55.3 %all_to_all.27 = bf16[1,2,128,4096]{2,1,0,3:T(2,128)(2,1)S(1)} all-to-all(bf16[1,2,128,4096]{2,1,0,3:T(2,128)(2,1)S(1)} %broadcast_select_fusion), channel_id=1, replica_groups=mesh['groups'=2,'member'=2,'fsdp'=8] {'fsdp'}, dimensions={3} | all-to-all | bytes 4194304 | tf_op jit(solution)/shard_map/all_to_all | solution.py:46
  67.1 3.2 reduce_sum.104
  70.3 0.0 all-gather.2.cloned.1.call-update
  70.3 0.0 reduce-scatter.2.cloned.1.call-start
  70.4 48.4 %all-gather.2.cloned.1.call-done = bf16[2,128,4096]{1,0,2:T(2,128)(2,1)} async-done(((bf16[2,128,512]{1,0,2:T(2,128)(2,1)}), bf16[2,128,4096]{1,0,2:T(2,128)(2,1)}) %all-gather.2.cloned.1.call-update) | async-done | bytes 2097168 | tf_op jit(solution)/shard_map/all_gather | solution.py:48
  118.8 5.4 multiply_reduce_fusion.2
  124.2 12.9 %multiply_convert_fusion.1 = bf16[2,128,4096]{1,0,2:T(2,128)(2,1)S(1)} fusion(f32[4096]{0:T(1024)S(1)} %bitcast.107, bf16[2,128,4096]{1,0,2:T(2,128)(2,1)} %all-gather.2.cloned.1.call-done, f32[2,128]{1,0:T(2,128)S(1)} %get-tuple-element.32), kind=kLoop, calls=%fused_computation.25 | loop fusion | flops 4194304 | bytes 4211712 | tf_op jit(solution)/shard_map/convert_element_type | solution.py:52
  137.1 0.0 slice-start
  137.1 8.4 %fusion.10 = f32[256,1792]{1,0:T(8,128)S(1)} fusion(bf16[1,4096,1792]{2,1,0:T(8,128)(2,1)} %param.17, bf16[512,8,2,128]{3,2,1,0:T(2,128)(2,1)S(1)} %bitcast.101), kind=kOutput, calls=%fused_computation.13 | convolution fusion | flops 3758096384 | bytes 18612224 | tf_op jit(solution)/shard_map/dot_general | solution.py:53
  145.5 0.0 slice-start.2
  145.5 11.3 %multiply_convert_fusion.4 = (bf16[256,1792]{1,0:T(8,128)(2,1)S(1)}, f32[256,1792]{1,0:T(8,128)}) fusion(f32[256,1792]{1,0:T(8,128)S(1)} %fusion.10, bf16[1,4096,1792]{2,1,0:T(8,128)(2,1)} %param.18, bf16[512,8,2,128]{3,2,1,0:T(2,128)(2,1)S(1)} %bitcast.102), kind=kOutput, calls=%fused_computation.37 | convolution fusion | flops 3760848896 | bytes 21364736 | tf_op jit(solution)/shard_map/dot_general | solution.py:54
  156.9 4.1 fusion.2
  161.0 0.6 collective-permute-start
  161.6 90.6 %collective-permute-done = f32[256,4096]{1,0:T(8,128)S(1)} collective-permute-done((f32[256,4096]{1,0:T(8,128)S(1)}, f32[256,4096]{1,0:T(8,128)S(1)}, u32[]{:S(2)}, u32[]{:S(2)}) %collective-permute-start) | collective-permute-done | bytes 4194336 | tf_op jit(solution)/shard_map/ppermute | solution.py:65
  252.2 0.6 add.139
  252.9 0.0 copy-start.8
  252.9 0.0 copy-start.9
  252.9 0.0 copy-start.10
  252.9 1.8 collective-permute-start.1
  254.7 88.8 %collective-permute-done.1 = f32[256,4096]{1,0:T(8,128)S(1)} collective-permute-done((f32[256,4096]{1,0:T(8,128)S(1)}, f32[256,4096]{1,0:T(8,128)S(1)}, u32[]{:S(2)}, u32[]{:S(2)}) %collective-permute-start.1) | collective-permute-done | bytes 4194336 | tf_op jit(solution)/shard_map/ppermute | solution.py:65
  343.5 2.5 add.140
  346.0 2.8 collective-permute-start.2
  348.9 4.6 copy.30
  353.5 0.0 copy-start.1
  353.5 173.7 %collective-permute-done.2 = f32[256,4096]{1,0:T(8,128)} collective-permute-done((f32[256,4096]{1,0:T(8,128)}, f32[256,4096]{1,0:T(8,128)}, u32[]{:S(2)}, u32[]{:S(2)}) %collective-permute-start.2) | collective-permute-done | bytes 4194336 | tf_op jit(solution)/shard_map/ppermute | solution.py:65
  527.3 5.3 multiply_reduce_fusion.1
  532.6 7.0 multiply_reduce_fusion
  539.6 0.1 bitcast_reduce_fusion
  539.7 0.1 multiply_reduce_fusion.7
  539.8 0.9 negate_multiply_fusion
  540.7 0.1 multiply_reduce_fusion.6
  540.8 0.7 fusion.33
  541.5 1.3 compare_select_fusion.1
  542.8 2.8 subtract_multiply_fusion
  545.6 12.5 %multiply_convert_fusion.2 = (bf16[256,1792]{1,0:T(8,128)(2,1)}, bf16[256,1792]{1,0:T(8,128)(2,1)}) fusion(f32[256,1792]{1,0:T(8,128)S(1)} %copy-done.5, f32[256,1792]{1,0:T(8,128)} %get-tuple-element.40, bf16[1,1792,4096]{2,1,0:T(8,128)(2,1)} %param.19, f32[256,4096]{1,0:T(8,128)} %subtract_multiply_fusion), kind=kOutput, calls=%fused_computation.35 | convolution fusion | flops 3765108736 | bytes 24379392 | tf_op jit(solution)/shard_map/dot_general | solution.py:25
  558.1 11.5 %fusion.4 = f32[256,4096]{1,0:T(8,128)} fusion(bf16[256,1792]{1,0:T(8,128)(2,1)} %get-tuple-element.27, bf16[1,4096,1792]{2,1,0:T(8,128)(2,1)} %param.18), kind=kOutput, calls=%fused_computation.7 | convolution fusion | flops 3758096384 | bytes 19791872 | tf_op jit(solution)/shard_map/dot_general | solution.py:25
  569.7 17.0 %fusion.15 = f32[256,4096]{1,0:T(8,128)} fusion(f32[256,4096]{1,0:T(8,128)} %fusion.4, bf16[256,1792]{1,0:T(8,128)(2,1)S(1)} %copy-done.6, bf16[1,4096,1792]{2,1,0:T(8,128)(2,1)} %param.17), kind=kOutput, calls=%fused_computation.18 | convolution fusion | flops 3759144960 | bytes 23986176 | tf_op jit(solution)/shard_map/dot_general | solution.py:25
  586.6 0.0 reduce-scatter.2.cloned.1.call-update
  586.7 0.6 copy-done.11
  587.3 88.2 %reduce-scatter.2.cloned.1.call-done = f32[256,512]{1,0:T(8,128)} async-done(((f32[256,4096]{1,0:T(8,128)}), f32[256,512]{1,0:T(8,128)}) %reduce-scatter.2.cloned.1.call-update) | async-done | bytes 524304 | tf_op jit(solution)/shard_map/reduce_scatter | solution.py:92
  675.5 2.0 multiply_reduce_fusion.3
  677.5 20.1 %psum.14 = f32[256]{0:T(256)S(1)} all-reduce(f32[256]{0:T(256)S(1)} %get-tuple-element.20), channel_id=1, replica_groups=mesh['groups'=2,'member'=2,'fsdp'=8] {'fsdp'}, use_global_device_ids=true, to_apply=%region_12.13 | all-reduce | flops 256 | bytes 2048 | tf_op jit(solution)/shard_map/psum | solution.py:95
  697.6 1.5 add_convert_fusion
  699.1 0.2 copy.31
  699.3 1.5 broadcast_select_fusion.1
  700.8 3.6 all-to-all-start.1
  704.5 0.0 all-reduce.2.cloned.1.call-start
  704.5 12.0 %fusion.12 = bf16[1,4096,1792]{2,1,0:T(8,128)(2,1)} fusion(bf16[256,1792]{1,0:T(8,128)(2,1)} %get-tuple-element.28, f32[256,4096]{1,0:T(8,128)} %get-tuple-element.26, f32[4096]{0:T(1024)S(1)} %bitcast.108), kind=kOutput, calls=%fused_computation.15 | convolution fusion | flops 3767533568 | bytes 19808256 | tf_op jit(solution)/shard_map/dot_general | solution.py:25
  716.5 33.1 %all-to-all-done.1 = bf16[8,2,128,512]{2,3,1,0:T(8,128)(2,1)S(1)} async-done(((bf16[8,2,128,512]{2,3,1,0:T(8,128)(2,1)}), bf16[8,2,128,512]{2,3,1,0:T(8,128)(2,1)S(1)}, u32[]{:S(2)}, u32[]{:S(2)}) %all-to-all-start.1) | async-done | bytes 2097184 | tf_op jit(solution)/shard_map/all_to_all | solution.py:106
  749.6 1.5 copy.32
  751.0 5.2 copy.33
  756.3 2.3 fusion.26
  758.6 2.1 copy.49
  760.7 0.0 all-reduce.2.cloned.1.call-update
  760.8 9.9 %fusion.14 = bf16[1,1792,4096]{2,1,0:T(8,128)(2,1)} fusion(bf16[256,1792]{1,0:T(8,128)(2,1)S(1)} %get-tuple-element.39, f32[256,4096]{1,0:T(8,128)} %subtract_multiply_fusion), kind=kOutput, calls=%fused_computation.17 | convolution fusion | flops 3766484992 | bytes 19791872 | tf_op jit(solution)/shard_map/dot_general | solution.py:25
  770.7 1.2 multiply_reduce_fusion.5
  771.9 1.3 dynamic-slice_multiply_fusion
  773.2 8.8 %fusion.13 = bf16[1,4096,1792]{2,1,0:T(8,128)(2,1)} fusion(bf16[256,1792]{1,0:T(8,128)(2,1)} %get-tuple-element.27, f32[256,4096]{1,0:T(8,128)S(1)} %copy-done, f32[4096]{0:T(1024)S(1)} %bitcast.109), kind=kOutput, calls=%fused_computation.16 | convolution fusion | flops 3767533568 | bytes 19808256 | tf_op jit(solution)/shard_map/dot_general | solution.py:25
  781.9 2.3 copy.51
  (38 shorter events, 0.2 us)
Async XLA Ops:
  7.2 111.6 %all-gather.2.cloned.1.call-start = ((), (), s32[]{:S(2)}) async-start(), calls=%async_computation.3 | async-start | bytes 2359296 | tf_op jit(solution)/shard_map/all_gather | solution.py:48
  11.8 112.4 %copy-start.7 = (f32[1,4096]{1,0:T(1,128)S(1)}, f32[1,4096]{1,0:T(1,128)}, u32[]{:S(2)}) copy-start(f32[1,4096]{1,0:T(1,128)} %param.14) | copy-start | bytes 49156
  70.3 605.2 %reduce-scatter.2.cloned.1.call-start = ((), (), s32[]{:S(2)}) async-start(), calls=%async_computation.4 | async-start | bytes 4718592 | tf_op jit(solution)/shard_map/reduce_scatter | solution.py:92
  137.1 19.8 %slice-start = ((s8[14680064]{0:T(1024)(128)(4,1)}), s8[4194304]{0:T(1024)(128)(4,1)S(1)}, s32[]{:S(2)}) async-start(s8[14680064]{0:T(1024)(128)(4,1)} %bitcast.120), calls=%async_computation.6 | async-start | bytes 8388608
  137.1 19.8 %slice-start.1 = ((s8[14680064]{0:T(1024)(128)(4,1)}), s8[4194304]{0:T(1024)(128)(4,1)S(1)}, s32[]{:S(2)}) async-start(s8[14680064]{0:T(1024)(128)(4,1)} %bitcast.120), calls=%async_computation.7 | async-start | bytes 8388608
  145.5 11.4 %copy-start.4 = (f32[256,1792]{1,0:T(8,128)}, f32[256,1792]{1,0:T(8,128)S(1)}, u32[]{:S(2)}) copy-start(f32[256,1792]{1,0:T(8,128)S(1)} %fusion.10) | copy-start | bytes 5505028
  145.5 11.4 %slice-start.2 = ((s8[14680064]{0:T(1024)(128)(4,1)}), s8[4194304]{0:T(1024)(128)(4,1)S(1)}, s32[]{:S(2)}) async-start(s8[14680064]{0:T(1024)(128)(4,1)} %bitcast.120), calls=%async_computation.8 | async-start | bytes 8388608
  145.5 11.4 %slice-start.3 = ((s8[14680064]{0:T(1024)(128)(4,1)}), s8[2097152]{0:T(1024)(128)(4,1)S(1)}, s32[]{:S(2)}) async-start(s8[14680064]{0:T(1024)(128)(4,1)} %bitcast.120), calls=%async_computation.9 | async-start | bytes 4194304
  161.0 91.3 %collective-permute-start = (f32[256,4096]{1,0:T(8,128)S(1)}, f32[256,4096]{1,0:T(8,128)S(1)}, u32[]{:S(2)}, u32[]{:S(2)}) collective-permute-start(f32[256,4096]{1,0:T(8,128)S(1)} %fusion.2), channel_id=1, source_target_pairs={{0,1},{1,0},{2,3},{3,2},{4,5},{5,4},{6,7},{7,6},{8,9},{9,8},{10,11... | collective-permute-start | bytes 12582920 | tf_op jit(solution)/shard_map/ppermute | solution.py:65
  252.9 96.0 %copy-start.8 = (f32[1,4096]{1,0:T(1,128)S(1)}, f32[1,4096]{1,0:T(1,128)}, u32[]{:S(2)}) copy-start(f32[1,4096]{1,0:T(1,128)} %param.15) | copy-start | bytes 49156
  252.9 95.9 %copy-start.9 = (f32[1,4096]{1,0:T(1,128)S(1)}, f32[1,4096]{1,0:T(1,128)}, u32[]{:S(2)}) copy-start(f32[1,4096]{1,0:T(1,128)} %param.16) | copy-start | bytes 49156
  252.9 96.0 %copy-start.10 = (s32[1,4,2]{1,2,0:T(2,128)S(1)}, s32[1,4,2]{1,2,0:T(2,128)}, u32[]{:S(2)}) copy-start(s32[1,4,2]{1,2,0:T(2,128)} %param.13) | copy-start | bytes 100
  252.9 96.0 %copy-start.3 = (bf16[2,128,4096]{1,0,2:T(2,128)(2,1)S(1)}, bf16[2,128,4096]{1,0,2:T(2,128)(2,1)}, u32[]{:S(2)}) copy-start(bf16[2,128,4096]{1,0,2:T(2,128)(2,1)} %all-gather.2.cloned.1.call-done) | copy-start | bytes 6291460
  252.9 90.6 %collective-permute-start.1 = (f32[256,4096]{1,0:T(8,128)S(1)}, f32[256,4096]{1,0:T(8,128)S(1)}, u32[]{:S(2)}, u32[]{:S(2)}) collective-permute-start(f32[256,4096]{1,0:T(8,128)S(1)} %add.139), channel_id=1, source_target_pairs={{0,2},{1,3},{2,0},{3,1},{4,6},{5,7},{6,4},{7,5},{8,10},{9,11},{10,... | collective-permute-start | bytes 12582920 | tf_op jit(solution)/shard_map/ppermute | solution.py:65
  346.0 181.2 %collective-permute-start.2 = (f32[256,4096]{1,0:T(8,128)}, f32[256,4096]{1,0:T(8,128)}, u32[]{:S(2)}, u32[]{:S(2)}) collective-permute-start(f32[256,4096]{1,0:T(8,128)} %add.140), channel_id=1, source_target_pairs={{0,4},{1,5},{2,6},{3,7},{4,0},{5,1},{6,2},{7,3},{8,12},{9,13},{10,... | collective-permute-start | bytes 12582920 | tf_op jit(solution)/shard_map/ppermute | solution.py:65
  353.5 179.0 %copy-start.1 = (f32[2,128,4096]{2,1,0:T(8,128)S(1)}, f32[2,128,4096]{2,1,0:T(8,128)}, u32[]{:S(2)}) copy-start(f32[2,128,4096]{2,1,0:T(8,128)} %copy.30) | copy-start | bytes 12582916
  539.6 6.0 copy-start.2
  542.8 2.8 copy-start.5
  558.1 11.5 %copy-start.6 = (bf16[256,1792]{1,0:T(8,128)(2,1)S(1)}, bf16[256,1792]{1,0:T(8,128)(2,1)}, u32[]{:S(2)}) copy-start(bf16[256,1792]{1,0:T(8,128)(2,1)} %get-tuple-element.28) | copy-start | bytes 2752516
  586.6 0.7 copy-start.11
  700.8 48.7 %all-to-all-start.1 = ((bf16[8,2,128,512]{2,3,1,0:T(8,128)(2,1)}), bf16[8,2,128,512]{2,3,1,0:T(8,128)(2,1)S(1)}, u32[]{:S(2)}, u32[]{:S(2)}) async-start(bf16[8,2,128,512]{2,3,1,0:T(8,128)(2,1)} %broadcast_select_fusion.1), calls=%async_computation.2 | async-start | bytes 4194304 | tf_op jit(solution)/shard_map/all_to_all | solution.py:106
  704.5 77.5 %all-reduce.2.cloned.1.call-start = ((), (), s32[]{:S(2)}) async-start(), calls=%async_computation.5 | async-start | bytes 2097152 | tf_op jit(solution)/shard_map/psum | solution.py:114
  760.8 12.4 %copy-start = (f32[256,4096]{1,0:T(8,128)S(1)}, f32[256,4096]{1,0:T(8,128)}, u32[]{:S(2)}) copy-start(f32[256,4096]{1,0:T(8,128)} %get-tuple-element.26) | copy-start | bytes 12582916
Sparse Core Ops, SparseCore 0:
  70.5 48.3 all-gather.1
  586.8 88.6 reduce-scatter.1
  760.9 18.4 all-reduce.1
